TPU v7x, 32 devices: a whole 2x2x4 slice. The times are simulated.
32 devices in a mesh: cell: 4 (over y, x), sub: 8 (over z, core).
Axes of the slice: x: 2, y: 2, z: 4, core: 2. Of those that a mesh axis runs over, the one named last changes fastest.
Arguments:
- shell_conc: float32 [4, 32, 10, 128, 128], P('cell', 'sub'), may hold values from 0.2 to 0.8
- heat_rise: float32 [4, 30, 128, 128], P('cell', None, 'sub'), may hold values from -5 to 5
- layer_current: float32 [4, 32, 128, 128], P('cell', 'sub'), may hold values from -4 to 4
- layer_counts: int32 [8], replicated, may hold values from 1 to 4, 30 in all
- contacts: int32 [4, 2], replicated, may hold values from -1 to 3, as said below
Outputs:
- conc_new: float32 [4, 32, 10, 128, 128], P('cell', 'sub')
- heat_new: float32 [4, 30, 128, 128], P('cell', None, 'sub')
Inputs may be any that keep to these rules, and one draw needn't show every extreme that they name: `layer_counts`: entry d is the number of consecutive layers held by index d of sub, in order; the entries sum to 30 and the largest is exactly 4. `contacts`: row c names the cell below and the cell above cell c in one stacking order of all 4 cells, each cell once; -1 marks the two ends of the stack.
All inputs are finite; a program needn't handle non-finite values.
Results may differ from a plain program's by a relative error of at most 0.0003.
Values sent between devices are 32-bit elements; how exact they have to be, the bound alone decides.
A program may use at most 64 MiB of HBM per device.

v0:
```python
import jax
import jax.numpy as jnp
from jax import lax
from jax.sharding import PartitionSpec as P

BASE_KELVIN = 298.15
RATE_ACTIVATION = 5000.0
DIFFUSION_ACTIVATION = 3000.0
RATE_CONSTANT = 0.5
VOLT_PER_KELVIN = 2.0 * 8.314462618 / 96485.33212
HEAT_SCALE = 10.0
ENTROPY_SLOPE = 0.001
DIFFUSION_STEP = 0.005
SURFACE_STEP = 0.005
INPLANE_CONDUCT = 0.25
THROUGH_CONDUCT = 2.0
CONTACT_CONDUCT = 0.5


def with_halo(cells, sides, width):
    for axis, dim in sides:
        count = lax.axis_size(axis)
        ends = count - 1
        head = lax.slice_in_dim(cells, 0, width, axis=dim)
        tail = lax.slice_in_dim(cells, cells.shape[dim] - width, cells.shape[dim], axis=dim)
        cells = jnp.concatenate(
            [
                lax.ppermute(tail, axis, [(i, (i + 1) % count) for i in range(ends)]),
                cells,
                lax.ppermute(head, axis, [((i + 1) % count, i) for i in range(ends)]),
            ],
            axis=dim,
        )
    return cells


def inverse_sine(value):
    magnitude = jnp.abs(value)
    rooted = jnp.sqrt(1.0 + magnitude * magnitude)
    positive = jnp.log1p(magnitude + magnitude * magnitude / (1.0 + rooted))
    return jnp.where(value < 0.0, -positive, positive)


def layer_tables(layer_counts, slot_count, layer_total):
    finish = jnp.cumsum(layer_counts)
    starts = finish - layer_counts
    devices = layer_counts.shape[0]
    device_ids = jnp.arange(devices, dtype=jnp.int32)
    slot_index = jnp.arange(devices * slot_count, dtype=jnp.int32)
    slot_owner = slot_index // slot_count
    slot_place = slot_index % slot_count
    owner_hits = slot_owner[:, None] == device_ids[None, :]
    owner_count = jnp.sum(jnp.where(owner_hits, layer_counts[None, :], 0), axis=1)
    owner_start = jnp.sum(jnp.where(owner_hits, starts[None, :], 0), axis=1)
    live_slot = slot_place < owner_count
    slot_layer = jnp.minimum(owner_start + slot_place, layer_total - 1)
    layer_index = jnp.arange(layer_total, dtype=jnp.int32)
    layer_owner = jnp.sum((finish[None, :] <= layer_index[:, None]).astype(jnp.int32), axis=1)
    layer_hits = layer_owner[:, None] == device_ids[None, :]
    layer_start = jnp.sum(jnp.where(layer_hits, starts[None, :], 0), axis=1)
    layer_slot = layer_owner * slot_count + layer_index - layer_start
    return (live_slot, slot_layer, layer_slot)


def kinetics(surface, kelvin, current):
    reciprocal = 1.0 / BASE_KELVIN - 1.0 / kelvin
    base_rate = (
        RATE_CONSTANT * jnp.exp(RATE_ACTIVATION * reciprocal) * jnp.sqrt(surface * (1.0 - surface))
    )
    ratio_rate = current / (2.0 * base_rate)
    arcsine = inverse_sine(ratio_rate)
    overvoltage = VOLT_PER_KELVIN * kelvin * arcsine
    entropic = ENTROPY_SLOPE * (0.5 - surface)
    source = HEAT_SCALE * current * (overvoltage + kelvin * entropic)
    heat_slope = (
        HEAT_SCALE
        * current
        * (
            VOLT_PER_KELVIN * arcsine
            - VOLT_PER_KELVIN
            * ratio_rate
            * RATE_ACTIVATION
            / (kelvin * jnp.sqrt(1.0 + ratio_rate * ratio_rate))
            + entropic
        )
    )
    return (source, heat_slope)


def particle(states, kelvin, current):
    shells = states.shape[1]
    speedup = jnp.exp(DIFFUSION_ACTIVATION * (1.0 / BASE_KELVIN - 1.0 / kelvin))
    volumes = [((radial + 1) ** 3 - radial**3) / (3.0 * shells**3) for radial in range(shells)]
    linkage = [
        DIFFUSION_STEP * speedup * ((radial + 1) ** 2 / shells**2 * shells)
        for radial in range(shells - 1)
    ]
    uppers = []
    values = []
    for radial in range(shells):
        diagonal = volumes[radial] + jnp.zeros_like(kelvin)
        right_side = volumes[radial] * states[:, radial]
        if radial < shells - 1:
            diagonal = diagonal + linkage[radial]
        else:
            right_side = right_side - SURFACE_STEP * current
        if radial > 0:
            diagonal = diagonal + linkage[radial - 1] - linkage[radial - 1] * uppers[radial - 1]
            right_side = right_side + linkage[radial - 1] * values[radial - 1]
        if radial < shells - 1:
            uppers.append(linkage[radial] / diagonal)
        else:
            uppers.append(jnp.zeros_like(kelvin))
        values.append(right_side / diagonal)
    result = [None] * shells
    result[shells - 1] = values[shells - 1]
    for radial in range(shells - 2, -1, -1):
        result[radial] = values[radial] + uppers[radial] * result[radial + 1]
    return jnp.stack(result, axis=1)


def column_solve(right_side, heat_slope):
    layer_total = right_side.shape[1]
    uppers = []
    values = []
    for height in range(layer_total):
        diagonal = 1.0 - heat_slope[:, height]
        source = right_side[:, height]
        if height > 0:
            diagonal = diagonal + THROUGH_CONDUCT - THROUGH_CONDUCT * uppers[height - 1]
            source = source + THROUGH_CONDUCT * values[height - 1]
        if height < layer_total - 1:
            diagonal = diagonal + THROUGH_CONDUCT
        uppers.append(THROUGH_CONDUCT / diagonal)
        values.append(source / diagonal)
    result = [None] * layer_total
    result[layer_total - 1] = values[layer_total - 1]
    for height in range(layer_total - 2, -1, -1):
        result[height] = values[height] + uppers[height] * result[height + 1]
    return jnp.stack(result, axis=1)


def per_device(shell_conc, heat_rise, layer_current, layer_counts, contacts):
    slot_count = shell_conc.shape[1]
    shells = shell_conc.shape[2]
    layer_total = heat_rise.shape[1]
    live_slot, slot_layer, layer_slot = layer_tables(layer_counts, slot_count, layer_total)
    position = lax.axis_index("sub")
    devices = lax.axis_size("sub")
    outgoing = jnp.take(heat_rise, slot_layer, axis=1)
    slot_rise = lax.all_to_all(outgoing, "sub", split_axis=1, concat_axis=2, tiled=True)
    kelvin = BASE_KELVIN + slot_rise
    surface = shell_conc[:, :, shells - 1]
    source, heat_slope = kinetics(surface, kelvin, layer_current)
    got_source, got_slope = (
        lax.all_to_all(source, "sub", split_axis=2, concat_axis=1, tiled=True),
        lax.all_to_all(heat_slope, "sub", split_axis=2, concat_axis=1, tiled=True),
    )
    layer_source = jnp.take(got_source, layer_slot, axis=1)
    layer_slope = jnp.take(got_slope, layer_slot, axis=1)
    updated = particle(shell_conc[0], kelvin[0], layer_current[0])[None]
    own_live = lax.dynamic_slice_in_dim(live_slot, position * slot_count, slot_count)
    conc_new = jnp.where(own_live[None, :, None, None, None], updated, 0.0)
    face_rows = jnp.stack([heat_rise[:, 0], heat_rise[:, layer_total - 1]], axis=1)
    every_face = lax.all_gather(face_rows, "cell", axis=0, tiled=True)
    partners = lax.dynamic_index_in_dim(contacts, lax.axis_index("cell"), 0, keepdims=False)
    lower_pair = lax.dynamic_index_in_dim(
        every_face, jnp.maximum(partners[0], 0), 0, keepdims=False
    )
    upper_pair = lax.dynamic_index_in_dim(
        every_face, jnp.maximum(partners[1], 0), 0, keepdims=False
    )
    below_face = jnp.where(partners[0] >= 0, lower_pair[1], 0.0)[None]
    above_face = jnp.where(partners[1] >= 0, upper_pair[0], 0.0)[None]
    rim_rows = with_halo(heat_rise, (("sub", 2),), 1)
    low_row = jnp.where(position == 0, heat_rise[:, :, 0:1], rim_rows[:, :, 0:1])
    high_row = jnp.where(position == devices - 1, heat_rise[:, :, -1:], rim_rows[:, :, -1:])
    column_pad = jnp.concatenate([low_row, heat_rise, high_row], axis=2)
    row_pad = jnp.pad(heat_rise, ((0, 0), (0, 0), (0, 0), (1, 1)), mode="edge")
    laplace = (
        column_pad[:, :, 2:]
        + column_pad[:, :, :-2]
        + row_pad[:, :, :, 2:]
        + row_pad[:, :, :, :-2]
        - 4.0 * heat_rise
    )
    right_side = heat_rise + INPLANE_CONDUCT * laplace + layer_source - layer_slope * heat_rise
    first_row = right_side[:, 0] + CONTACT_CONDUCT * (below_face - heat_rise[:, 0])
    last_row = right_side[:, layer_total - 1] + CONTACT_CONDUCT * (
        above_face - heat_rise[:, layer_total - 1]
    )
    right_side = jnp.concatenate(
        [first_row[:, None], right_side[:, 1 : layer_total - 1], last_row[:, None]], axis=1
    )
    heat_new = column_solve(right_side, layer_slope)
    return (conc_new, heat_new)


def solution(mesh):
    in_specs = (
        P("cell", "sub", None, None, None),
        P("cell", None, "sub", None),
        P("cell", "sub", None, None),
        P(),
        P(),
    )
    out_specs = (P("cell", "sub", None, None, None), P("cell", None, "sub", None))
    return jax.shard_map(
        per_device, mesh=mesh, in_specs=in_specs, out_specs=out_specs, check_vma=False
    )
```

profile of v0, /device:TPU:0, one launch (start us, length us, event | category | flops | bytes accessed | tf_op | source)
XLA Modules:
  0.0 71.9 jit_solution(17056215816559929877)
XLA Ops:
  0.6 0.0 copy-start
  0.6 1.0 %fusion.193 = (f32[1,30,1,128]{3,2,1,0:T(1,128)S(1)}, f32[1,30,1,128]{3,2,1,0:T(1,128)S(1)}) fusion(f32[1,30,16,128]{3,2,1,0:T(8,128)} %param.8), kind=kLoop, calls=%fused_computation.427 | loop fusion | bytes 61440 | tf_op jit(solution)/shard_map/slice | solution.py:176
  1.6 1.3 %collective-permute-start = (f32[1,30,1,128]{3,2,1,0:T(1,128)S(1)}, f32[1,30,1,128]{3,2,1,0:T(1,128)S(1)}, u32[]{:S(2)}, u32[]{:S(2)}) collective-permute-start(f32[1,30,1,128]{3,2,1,0:T(1,128)S(1)} %get-tuple-element.86), channel_id=1, source_target_pairs={{1,0},{2,1},{3,2},{4,3},{5,4},{6,5},{7,6},{9,8},{10,9},{11,10},{12... | collective-permute-start | bytes 46088 | tf_op jit(solution)/shard_map/ppermute | solution.py:30
  2.9 3.0 %collective-permute-start.1 = (f32[1,30,1,128]{3,2,1,0:T(1,128)S(1)}, f32[1,30,1,128]{3,2,1,0:T(1,128)S(1)}, u32[]{:S(2)}, u32[]{:S(2)}) collective-permute-start(f32[1,30,1,128]{3,2,1,0:T(1,128)S(1)} %get-tuple-element.87), channel_id=1, source_target_pairs={{0,1},{1,2},{2,3},{3,4},{4,5},{5,6},{6,7},{8,9},{9,10},{10,11},{11... | collective-permute-start | bytes 46088 | tf_op jit(solution)/shard_map/ppermute | solution.py:28
  6.0 0.8 %reduce-window.8 = s32[8,1]{0,1:T(1,128)S(1)} reduce-window(s32[8,1]{0,1:T(1,128)} %bitcast.460, s32[]{:T(128)} %constant.160.clone.1), window={size=8x1 pad=7_0x0_0}, to_apply=%region_1.2 | reduce-window | flops 56 | bytes 68 | tf_op jit(solution)/shard_map/reduce-window.3
  6.8 0.7 bitcast_subtract_fusion
  7.5 0.7 %select_reduce_fusion.2 = (s32[32]{0:T(128)S(1)}, s32[32]{0:T(128)S(1)}) fusion(s32[8]{0:T(128)} %param.10, s32[32]{0:T(128)S(1)} %and_select_fusion.1, s32[8]{0:T(128)S(1)} %bitcast_subtract_fusion), kind=kLoop, calls=%fused_computation.407 | loop fusion | flops 1216 | bytes 448 | tf_op jit(solution)/shard_map/reduce_sum | solution.py:53
  8.3 1.5 %gather_fusion = f32[32,16,128]{2,1,0:T(8,128)S(1)} fusion(f32[30,16,128]{2,1,0:T(8,128)} %bitcast.445, s32[1024]{0:T(1024)S(1)} %pad_clamp_fusion.1), kind=kCustom, calls=%fused_computation.2 | custom fusion | bytes 524416 | tf_op jit(solution)/shard_map/jit(_take)/gather | solution.py:150
  9.8 0.8 %bitcast_select_fusion = f32[1,32,16,128]{3,2,0,1:T(8,128)} fusion(f32[32,16,128]{2,1,0:T(8,128)S(1)} %gather_fusion, pred[32]{0:T(512)(128)(4,1)S(1)} %compare_and_fusion.1), kind=kLoop, calls=%fused_computation.119 | loop fusion | flops 65536 | bytes 524320 | tf_op jit(solution)/shard_map/jit(_take)/select_n | solution.py:150
  10.6 6.4 %all-to-all-start = ((f32[1,32,16,128]{3,2,0,1:T(8,128)}), f32[1,32,16,128]{3,2,0,1:T(8,128)S(1)}, u32[]{:S(2)}, u32[]{:S(2)}) async-start(f32[1,32,16,128]{3,2,0,1:T(8,128)} %bitcast_select_fusion), calls=%async_computation | async-start | bytes 524288 | tf_op jit(solution)/shard_map/all_to_all | solution.py:151
  16.9 0.7 fusion.195
  17.7 1.9 %fusion.194 = (f32[1,30,16,1]{3,2,1,0:T(8,128)}, f32[1,30,16,1]{3,2,1,0:T(8,128)}) fusion(f32[1,30,16,128]{3,2,1,0:T(8,128)} %param.8), kind=kLoop, calls=%fused_computation.428 | loop fusion | bytes 7680 | tf_op jit(solution)/shard_map/jit(_pad)/slice | solution.py:179
  19.6 0.1 convert_reduce_fusion
  19.6 0.1 select_reduce_fusion
  19.8 0.0 copy-done
  19.8 0.1 constant_dynamic-slice_fusion
  19.8 0.5 fusion.196
  22.9 0.0 copy-start.1
  22.9 2.0 %copy.155 = f32[1,4,10,128,128]{4,3,1,2,0:T(8,128)S(1)} copy(f32[1,4,10,128,128]{4,3,2,1,0:T(8,128)} %param.7) | data formatting | bytes 5242880 | tf_op args[0]
  24.9 0.1 dynamic_slice.14
  25.0 8.2 %all_gather.3 = f32[4,2,16,128]{3,2,1,0:T(8,128)S(1)} all-gather(f32[1,2,16,128]{3,2,1,0:T(8,128)S(1)} %pad_maximum_fusion.4), channel_id=1, replica_groups=mesh['cell'=4,'sub'=8] {'cell'}, dimensions={0}, use_global_device_ids=true | all-gather | bytes 81920 | tf_op jit(solution)/shard_map/all_gather | solution.py:165
  33.2 0.0 collective-permute-done
  33.2 0.0 collective-permute-done.1
  33.2 0.0 copy-done.1
  33.3 0.0 all-to-all-done
  33.3 0.3 broadcast_add_fusion
  33.6 0.0 copy-start.9
  33.6 0.7 copy.129
  34.4 0.7 %copy.130 = f32[1,4,8,16,128]{4,3,2,1,0:T(8,128)} copy(f32[1,4,8,16,128]{4,3,1,2,0:T(8,128)S(1)} %bitcast.453) | data formatting | bytes 524288 | tf_op jit(solution)/shard_map/mul | solution.py:95
  35.1 0.7 copy.131
  35.8 0.7 %copy.132 = f32[1,4,8,16,128]{4,3,2,1,0:T(8,128)} copy(f32[1,4,8,16,128]{4,3,1,2,0:T(8,128)S(1)} %bitcast.451) | data formatting | bytes 524288 | tf_op jit(solution)/shard_map/mul | solution.py:95
  36.5 0.7 %copy.133 = f32[1,4,8,16,128]{4,3,2,1,0:T(8,128)} copy(f32[1,4,8,16,128]{4,3,1,2,0:T(8,128)S(1)} %bitcast.450) | data formatting | bytes 524288 | tf_op jit(solution)/shard_map/mul | solution.py:95
  37.2 0.7 copy.134
  38.0 0.7 copy.135
  38.7 0.0 copy-done.9
  38.7 1.3 %fusion.33 = (f32[1,4,128,128]{3,2,1,0:T(8,128)S(1)}, f32[1,4,128,128]{3,2,1,0:T(8,128)}) fusion(f32[1,8,4,16,128]{4,3,1,2,0:T(8,128)S(1)} %copy.145, f32[1,4,128,128]{3,2,1,0:T(8,128)S(1)} %copy-done.9, f32[1,4,10,128,128]{4,3,1,2,0:T(8,128)S(1)} %copy.155), kind=kLoop, calls=%fused_computation.65 | loop fusion | flops 2162688 | bytes 1310720 | tf_op jit(solution)/shard_map/mul | solution.py:76
  39.9 0.9 %copy.150 = f32[1,4,128,128]{3,1,0,2:T(4,128)} copy(f32[1,4,128,128]{3,2,1,0:T(8,128)S(1)} %get-tuple-element.66) | data formatting | bytes 524288 | tf_op jit(solution)/shard_map/mul | solution.py:76
  40.8 5.1 %all-to-all-start.2 = ((f32[1,4,128,128]{3,1,0,2:T(4,128)}), f32[1,4,128,128]{3,1,0,2:T(4,128)}, u32[]{:S(2)}, u32[]{:S(2)}) async-start(f32[1,4,128,128]{3,1,0,2:T(4,128)} %copy.150), calls=%async_computation.2 | async-start | bytes 524288 | tf_op jit(solution)/shard_map/all_to_all | solution.py:157
  45.9 1.8 %copy.147 = f32[1,4,128,128]{3,1,0,2:T(4,128)} copy(f32[1,4,128,128]{3,2,1,0:T(8,128)} %get-tuple-element.67) | data formatting | bytes 524288 | tf_op jit(solution)/shard_map/mul | solution.py:74
  47.7 0.0 copy-start.6
  47.8 0.0 copy-start.7
  47.8 0.0 copy-start.10
  47.8 0.0 copy-start.11
  47.8 2.2 %fusion.10 = (f32[4,1,128,128]{3,2,0,1:T(8,128)S(1)}, f32[4,1,128,128]{3,2,0,1:T(8,128)S(1)}, f32[4,1,128,128]{3,2,0,1:T(8,128)S(1)}, f32[4,1,128,128]{3,2,0,1:T...) fusion(f32[4,10,128,128]{3,2,0,1:T(8,128)S(1)} %bitcast.443, ...), kind=kLoop, calls=%fused_computation.22 | loop fusion | flops 4325376 | bytes 7077888 | tf_op jit(solution)/shard_map/div | solution.py:114
  50.0 0.0 copy-done.2
  50.0 0.0 copy-done.3
  50.0 0.0 copy-done.4
  50.0 0.0 copy-done.5
  50.0 0.0 copy-done.6
  50.1 0.7 multiply_add_fusion.1
  50.7 0.0 copy-start.8
  51.1 0.4 copy-done.8
  51.5 4.2 %all-to-all-done.2 = f32[1,4,128,128]{3,1,0,2:T(4,128)} async-done(((f32[1,4,128,128]{3,1,0,2:T(4,128)}), f32[1,4,128,128]{3,1,0,2:T(4,128)}, u32[]{:S(2)}, u32[]{:S(2)}) %all-to-all-start.2) | async-done | bytes 262176 | tf_op jit(solution)/shard_map/all_to_all | solution.py:157
  55.7 3.4 %all-to-all-start.1 = ((f32[1,4,128,128]{3,1,0,2:T(4,128)}), f32[1,4,128,128]{3,1,0,2:T(4,128)S(1)}, u32[]{:S(2)}, u32[]{:S(2)}) async-start(f32[1,4,128,128]{3,1,0,2:T(4,128)} %copy.147), calls=%async_computation.1 | async-start | bytes 524288 | tf_op jit(solution)/shard_map/all_to_all | solution.py:156
  59.1 1.0 %bitcast_dynamic-update-slice_fusion.9 = f32[1,4,10,128,128]{4,3,2,1,0:T(8,128)S(1)} fusion(f32[1,4,10,128,128]{4,3,2,1,0:T(8,128)S(1)} %bitcast_dynamic-update-slice_fusion, f32[4,1,128,128]{3,2,0,1:T(8,128)} %copy-done.8), kind=kLoop, calls=%fused_computation.66 | loop fusion | bytes 524288 | tf_op jit(solution)/shard_map/stack | solution.py:119
  60.1 1.8 %broadcast_select_fusion = f32[1,4,10,128,128]{4,3,2,1,0:T(8,128)} fusion(f32[1,4,10,128,128]{4,3,2,1,0:T(8,128)S(1)} %bitcast_dynamic-update-slice_fusion.9, pred[4]{0:T(512)(128)(4,1)S(1)} %dynamic_slice.14), kind=kLoop, calls=%fused_computation.3 | loop fusion | flops 655360 | bytes 5242884 | tf_op jit(solution)/shard_map/jit(_where)/select_n | solution.py:163
  62.0 1.0 %copy.151 = f32[1,4,128,128]{3,2,1,0:T(8,128)S(1)} copy(f32[1,4,128,128]{3,1,0,2:T(4,128)} %all-to-all-done.2) | data formatting | bytes 524288 | tf_op jit(solution)/shard_map/all_to_all | solution.py:157
  63.0 5.8 %all-to-all-done.1 = f32[1,4,128,128]{3,1,0,2:T(4,128)S(1)} async-done(((f32[1,4,128,128]{3,1,0,2:T(4,128)}), f32[1,4,128,128]{3,1,0,2:T(4,128)S(1)}, u32[]{:S(2)}, u32[]{:S(2)}) %all-to-all-start.1) | async-done | bytes 262176 | tf_op jit(solution)/shard_map/all_to_all | solution.py:156
  68.8 0.6 gather_fusion.2
  69.4 0.6 gather_fusion.1
  70.0 0.3 bitcast_select_fusion.1
  70.4 0.4 constant_dynamic-update-slice_fusion.29
  71.2 0.0 copy-start.14
  71.2 0.7 copy-done.14
  (64 shorter events, 0.7 us)
Async XLA Ops:
  0.6 19.1 %copy-start = (s32[4,2]{0,1:T(2,128)S(1)}, s32[4,2]{0,1:T(2,128)}, u32[]{:S(2)}) copy-start(s32[4,2]{0,1:T(2,128)} %param.11) | copy-start | bytes 100
  1.6 31.6 %collective-permute-start = (f32[1,30,1,128]{3,2,1,0:T(1,128)S(1)}, f32[1,30,1,128]{3,2,1,0:T(1,128)S(1)}, u32[]{:S(2)}, u32[]{:S(2)}) collective-permute-start(f32[1,30,1,128]{3,2,1,0:T(1,128)S(1)} %get-tuple-element.86), channel_id=1, source_target_pairs={{1,0},{2,1},{3,2},{4,3},{5,4},{6,5},{7,6},{9,8},{10,9},{11,10},{12... | collective-permute-start | bytes 46088 | tf_op jit(solution)/shard_map/ppermute | solution.py:30
  2.9 30.3 %collective-permute-start.1 = (f32[1,30,1,128]{3,2,1,0:T(1,128)S(1)}, f32[1,30,1,128]{3,2,1,0:T(1,128)S(1)}, u32[]{:S(2)}, u32[]{:S(2)}) collective-permute-start(f32[1,30,1,128]{3,2,1,0:T(1,128)S(1)} %get-tuple-element.87), channel_id=1, source_target_pairs={{0,1},{1,2},{2,3},{3,4},{4,5},{5,6},{6,7},{8,9},{9,10},{10,11},{11... | collective-permute-start | bytes 46088 | tf_op jit(solution)/shard_map/ppermute | solution.py:28
  10.6 22.7 %all-to-all-start = ((f32[1,32,16,128]{3,2,0,1:T(8,128)}), f32[1,32,16,128]{3,2,0,1:T(8,128)S(1)}, u32[]{:S(2)}, u32[]{:S(2)}) async-start(f32[1,32,16,128]{3,2,0,1:T(8,128)} %bitcast_select_fusion), calls=%async_computation | async-start | bytes 524288 | tf_op jit(solution)/shard_map/all_to_all | solution.py:151
  22.9 10.3 %copy-start.1 = (f32[1,30,16,128]{3,2,1,0:T(8,128)S(1)}, f32[1,30,16,128]{3,2,1,0:T(8,128)}, u32[]{:S(2)}) copy-start(f32[1,30,16,128]{3,2,1,0:T(8,128)} %param.8) | copy-start | bytes 737284
  33.6 5.1 %copy-start.9 = (f32[1,4,128,128]{3,2,1,0:T(8,128)S(1)}, f32[1,4,128,128]{3,2,1,0:T(8,128)}, u32[]{:S(2)}) copy-start(f32[1,4,128,128]{3,2,1,0:T(8,128)} %param.9) | copy-start | bytes 786436
  40.8 14.9 %all-to-all-start.2 = ((f32[1,4,128,128]{3,1,0,2:T(4,128)}), f32[1,4,128,128]{3,1,0,2:T(4,128)}, u32[]{:S(2)}, u32[]{:S(2)}) async-start(f32[1,4,128,128]{3,1,0,2:T(4,128)} %copy.150), calls=%async_computation.2 | async-start | bytes 524288 | tf_op jit(solution)/shard_map/all_to_all | solution.py:157
  47.7 2.3 %copy-start.2 = (f32[1,4,8,16,128]{4,3,2,1,0:T(8,128)S(1)}, f32[1,4,8,16,128]{4,3,2,1,0:T(8,128)}, u32[]{:S(2)}) copy-start(f32[1,4,8,16,128]{4,3,2,1,0:T(8,128)} %copy.129) | copy-start | bytes 786436
  47.7 2.3 %copy-start.3 = (f32[1,4,8,16,128]{4,3,2,1,0:T(8,128)S(1)}, f32[1,4,8,16,128]{4,3,2,1,0:T(8,128)}, u32[]{:S(2)}) copy-start(f32[1,4,8,16,128]{4,3,2,1,0:T(8,128)} %copy.130) | copy-start | bytes 786436
  47.7 2.3 %copy-start.4 = (f32[1,4,8,16,128]{4,3,2,1,0:T(8,128)S(1)}, f32[1,4,8,16,128]{4,3,2,1,0:T(8,128)}, u32[]{:S(2)}) copy-start(f32[1,4,8,16,128]{4,3,2,1,0:T(8,128)} %copy.131) | copy-start | bytes 786436
  47.7 2.3 %copy-start.5 = (f32[1,4,8,16,128]{4,3,2,1,0:T(8,128)S(1)}, f32[1,4,8,16,128]{4,3,2,1,0:T(8,128)}, u32[]{:S(2)}) copy-start(f32[1,4,8,16,128]{4,3,2,1,0:T(8,128)} %copy.132) | copy-start | bytes 786436
  47.7 2.3 %copy-start.6 = (f32[1,4,8,16,128]{4,3,2,1,0:T(8,128)S(1)}, f32[1,4,8,16,128]{4,3,2,1,0:T(8,128)}, u32[]{:S(2)}) copy-start(f32[1,4,8,16,128]{4,3,2,1,0:T(8,128)} %copy.133) | copy-start | bytes 786436
  47.8 2.3 %copy-start.7 = (f32[1,4,8,16,128]{4,3,2,1,0:T(8,128)S(1)}, f32[1,4,8,16,128]{4,3,2,1,0:T(8,128)}, u32[]{:S(2)}) copy-start(f32[1,4,8,16,128]{4,3,2,1,0:T(8,128)} %copy.134) | copy-start | bytes 786436
  47.8 2.3 %copy-start.10 = (f32[1,4,128,128]{3,2,1,0:T(8,128)S(1)}, f32[1,4,128,128]{3,2,1,0:T(8,128)}, u32[]{:S(2)}) copy-start(f32[1,4,128,128]{3,2,1,0:T(8,128)} %param.9) | copy-start | bytes 786436
  47.8 2.3 %copy-start.11 = (f32[1,4,8,16,128]{4,3,2,1,0:T(8,128)S(1)}, f32[1,4,8,16,128]{4,3,2,1,0:T(8,128)}, u32[]{:S(2)}) copy-start(f32[1,4,8,16,128]{4,3,2,1,0:T(8,128)} %copy.135) | copy-start | bytes 786436
  50.7 0.7 copy-start.8
  55.7 13.1 %all-to-all-start.1 = ((f32[1,4,128,128]{3,1,0,2:T(4,128)}), f32[1,4,128,128]{3,1,0,2:T(4,128)S(1)}, u32[]{:S(2)}, u32[]{:S(2)}) async-start(f32[1,4,128,128]{3,1,0,2:T(4,128)} %copy.147), calls=%async_computation.1 | async-start | bytes 524288 | tf_op jit(solution)/shard_map/all_to_all | solution.py:156
  62.0 8.1 %copy-start.12 = (f32[1,30,16,1]{3,2,1,0:T(8,128)S(1)}, f32[1,30,16,1]{3,2,1,0:T(8,128)}, u32[]{:S(2)}) copy-start(f32[1,30,16,1]{3,2,1,0:T(8,128)} %get-tuple-element.88) | copy-start | bytes 5764
  62.0 8.1 %copy-start.13 = (f32[1,30,16,1]{3,2,1,0:T(8,128)S(1)}, f32[1,30,16,1]{3,2,1,0:T(8,128)}, u32[]{:S(2)}) copy-start(f32[1,30,16,1]{3,2,1,0:T(8,128)} %get-tuple-element.89) | copy-start | bytes 5764
  71.2 0.7 copy-start.14
where the time goes:
time: 72.6 us; the launch traced here: 71.9 us
  local copies, waits for them, and re-layouts  20 us (28%)
  starting transfers between devices  19.2 us (26%)
  other arithmetic  10.6 us (15%)
  waiting for transfers between devices  10 us (14%)
  blocking collectives  8.23 us (11%)
  between operations  3.8 us (5%)
    all_gather x1, blocking collectives, per_device(): every_face = lax.all_gather(face_rows, 'cell', axis=0, tiled=True)  8.23 us
    all_to_all x1, starting transfers between devices, per_device(): lax.all_to_all(outgoing, 'sub', split_axis=1, concat_axis=2, tiled=True)  6.35 us
    all_to_all x1, waiting for transfers between devices, per_device(): lax.all_to_all(source, 'sub', split_axis=2, concat_axis=1, tiled=True)  5.76 us
    all_to_all x1, starting transfers between devices, per_device(): lax.all_to_all(heat_slope, 'sub', split_axis=2, concat_axis=1, tiled=True)  5.1 us
    mul x9, local copies, waits for them, and re-layouts, particle(): DIFFUSION_STEP * speedup * ((radial + 1) ** 2 / shells ** 2 * shells)  5.07 us
    all_to_all x1, waiting for transfers between devices, per_device(): lax.all_to_all(heat_slope, 'sub', split_axis=2, concat_axis=1, tiled=True)  4.23 us
    all_to_all x1, starting transfers between devices, per_device(): lax.all_to_all(source, 'sub', split_axis=2, concat_axis=1, tiled=True)  3.41 us
    unnamed x50, local copies, waits for them, and re-layouts  3.22 us
  transfers between devices with their start and end apart: 5, of which 2 were waited for; matrix products, arithmetic and copies ran while one was open for 26% of the time, Pallas kernels for 0%

commit v1 on v0

v1 whole, which is shorter than its diff:
```python
import functools

import jax
import jax.numpy as jnp
from jax import lax
from jax.experimental import pallas as pl
from jax.experimental.pallas import tpu as pltpu
from jax.sharding import PartitionSpec as P

BASE_KELVIN = 298.15
RATE_ACTIVATION = 5000.0
DIFFUSION_ACTIVATION = 3000.0
RATE_CONSTANT = 0.5
VOLT_PER_KELVIN = 2.0 * 8.314462618 / 96485.33212
HEAT_SCALE = 10.0
ENTROPY_SLOPE = 0.001
DIFFUSION_STEP = 0.005
SURFACE_STEP = 0.005
INPLANE_CONDUCT = 0.25
THROUGH_CONDUCT = 2.0
CONTACT_CONDUCT = 0.5
MESH = pl.DeviceIdType.MESH


def partner(me, offset):
    bit = 1
    result = me
    while bit <= offset:
        if offset & bit:
            result = result + bit * (1 - 2 * ((me // bit) % 2))
        bit *= 2
    return result


def peer_of(me, offset, count):
    if count & (count - 1) == 0:
        return partner(me, offset)
    return (me + offset) % count


def inverse_sine(value):
    magnitude = jnp.abs(value)
    rooted = jnp.sqrt(1.0 + magnitude * magnitude)
    positive = jnp.log1p(magnitude + magnitude * magnitude / (1.0 + rooted))
    return jnp.where(value < 0.0, -positive, positive), rooted


def kinetics(surface, rise, current):
    kelvin = BASE_KELVIN + rise
    per_kelvin = 1.0 / kelvin
    reciprocal = rise * (1.0 / BASE_KELVIN) * per_kelvin
    ratio_rate = (
        current
        * jnp.exp(-RATE_ACTIVATION * reciprocal)
        * lax.rsqrt(surface * (1.0 - surface))
        * (0.5 / RATE_CONSTANT)
    )
    arcsine, rooted = inverse_sine(ratio_rate)
    entropic = ENTROPY_SLOPE * (0.5 - surface)
    scaled = HEAT_SCALE * current
    common = VOLT_PER_KELVIN * arcsine + entropic
    source = scaled * kelvin * common
    heat_slope = scaled * (
        common - (VOLT_PER_KELVIN * RATE_ACTIVATION) * ratio_rate * per_kelvin / rooted
    )
    return source, heat_slope


def kernel(
    cells, subs,
    counts, contacts, heat, conc, current,
    conc_new, heat_new,
    staged, slot_rise, conc_in, current_in, surface_rows, current_rows,
    low_edge, high_edge, faces, base, extra, diagonal, layer_slot,
    own_sem, heat_send, heat_recv, surf_send, surf_recv, curr_send, curr_recv,
    edge_send, edge_recv, face_send, face_recv, out_sem,
):
    cell = lax.axis_index("cell")
    sub = lax.axis_index("sub")
    slots, shells, gy, gx = conc_in.shape
    layers, rows, _ = heat.shape[1:]

    offsets = list(range(1, subs))
    far_first = offsets[::-1]

    def at_sub(index):
        return (cell, index)

    barrier = pltpu.get_barrier_semaphore()
    for offset in offsets:
        pl.semaphore_signal(
            barrier, inc=1, device_id=at_sub(peer_of(sub, offset, subs)), device_id_type=MESH
        )
    for offset in range(1, cells):
        pl.semaphore_signal(
            barrier, inc=1, device_id=(peer_of(cell, offset, cells), sub), device_id_type=MESH
        )

    loads = [
        pltpu.make_async_copy(current.at[0], current_in, own_sem.at[0]),
        pltpu.make_async_copy(conc.at[0], conc_in, own_sem.at[1]),
    ]
    for load in loads:
        load.start()

    start = jnp.int32(0)
    for index in range(subs):
        held = counts[index]
        for place in range(slots):
            layer = jnp.minimum(start + place, layers - 1)
            staged[index * slots + place] = heat[0, layer]
        start = start + held
    faces[cell] = jnp.zeros((2, rows, gx), jnp.float32)

    def slot_of(layer, carry):
        total = jnp.int32(0)
        slot = layer
        for index in range(subs):
            total = total + counts[index]
            slot = slot + jnp.where(total <= layer, slots - counts[index], 0)
        layer_slot[layer] = jnp.minimum(slot, subs * slots - 1)
        return carry

    pl.semaphore_wait(barrier, subs - 1 + cells - 1)

    sends = []

    def rows_of(index):
        return pl.ds(pl.multiple_of(index * rows, rows), rows)

    def slots_of(index):
        return pl.ds(index * slots, slots)

    def heat_copy(source, target, device):
        return pltpu.make_async_remote_copy(
            src_ref=staged.at[slots_of(target)],
            dst_ref=slot_rise.at[:, rows_of(source)],
            send_sem=heat_send.at[target],
            recv_sem=heat_recv.at[source],
            device_id=at_sub(device),
            device_id_type=MESH,
        )

    def surf_copy(source, target, device):
        return pltpu.make_async_remote_copy(
            src_ref=conc.at[0, :, shells - 1, rows_of(target)],
            dst_ref=surface_rows.at[slots_of(source)],
            send_sem=surf_send.at[target],
            recv_sem=surf_recv.at[source],
            device_id=at_sub(device),
            device_id_type=MESH,
        )

    def curr_copy(source, target, device):
        return pltpu.make_async_remote_copy(
            src_ref=current.at[0, :, rows_of(target)],
            dst_ref=current_rows.at[slots_of(source)],
            send_sem=curr_send.at[target],
            recv_sem=curr_recv.at[source],
            device_id=at_sub(device),
            device_id_type=MESH,
        )

    for offset in far_first:
        other = peer_of(sub, offset, subs)
        copy = heat_copy(sub, other, other)
        copy.start()
        sends.append(copy)

    to_below = pltpu.make_async_remote_copy(
        src_ref=heat.at[0, :, pl.ds(0, 1)],
        dst_ref=high_edge,
        send_sem=edge_send.at[0],
        recv_sem=edge_recv.at[0],
        device_id=at_sub(jnp.maximum(sub - 1, 0)),
        device_id_type=MESH,
    )
    to_above = pltpu.make_async_remote_copy(
        src_ref=heat.at[0, :, pl.ds(rows - 1, 1)],
        dst_ref=low_edge,
        send_sem=edge_send.at[1],
        recv_sem=edge_recv.at[1],
        device_id=at_sub(jnp.minimum(sub + 1, subs - 1)),
        device_id_type=MESH,
    )

    @pl.when(sub > 0)
    def _():
        to_below.start()

    @pl.when(sub < subs - 1)
    def _():
        to_above.start()

    def face_copies(source, device):
        return [
            pltpu.make_async_remote_copy(
                src_ref=heat.at[0, layer],
                dst_ref=faces.at[source, place],
                send_sem=face_send.at[2 * device + place],
                recv_sem=face_recv.at[2 * source + place],
                device_id=(device, sub),
                device_id_type=MESH,
            )
            for place, layer in ((0, 0), (1, layers - 1))
        ]

    for offset in range(1, cells):
        for copy in face_copies(cell, peer_of(cell, offset, cells)):
            copy.start()
            sends.append(copy)

    for offset in far_first:
        other = peer_of(sub, offset, subs)
        for copy in (surf_copy(sub, other, other), curr_copy(sub, other, other)):
            copy.start()
            sends.append(copy)
    mine = [
        pltpu.make_async_copy(
            conc.at[0, :, shells - 1, rows_of(sub)], surface_rows.at[slots_of(sub)], own_sem.at[2]
        ),
        pltpu.make_async_copy(
            current.at[0, :, rows_of(sub)], current_rows.at[slots_of(sub)], own_sem.at[3]
        ),
    ]
    for copy in mine:
        copy.start()
    slot_rise[:, rows_of(sub)] = staged[slots_of(sub)]

    lax.fori_loop(0, layers, slot_of, jnp.int32(0))

    live_count = counts[sub]
    live = lax.broadcasted_iota(jnp.int32, (slots, rows, gx), 0) < live_count
    volumes = [((r + 1) ** 3 - r**3) / (3.0 * shells**3) for r in range(shells)]
    weights = [DIFFUSION_STEP * ((r + 1) ** 2 / shells**2 * shells) for r in range(shells - 1)]

    def particle(where):
        rise = slot_rise[:, where]
        speedup = jnp.exp(
            (DIFFUSION_ACTIVATION / BASE_KELVIN) * rise / (BASE_KELVIN + rise)
        )
        uppers = []
        values = []
        link = None
        for r in range(shells):
            right = volumes[r] * conc_in[:, r, where]
            if r == shells - 1:
                right = right - SURFACE_STEP * current_in[:, where]
            pivot = volumes[r]
            if r > 0:
                pivot = pivot + link * (1.0 - uppers[r - 1])
                right = right + link * values[r - 1]
            if r < shells - 1:
                next_link = weights[r] * speedup
                pivot = pivot + next_link
            inverse = 1.0 / pivot
            if r < shells - 1:
                uppers.append(next_link * inverse)
                link = next_link
            values.append(right * inverse)
        result = values[shells - 1]
        conc_in[:, shells - 1, where] = jnp.where(live, result, 0.0)
        for r in range(shells - 2, -1, -1):
            result = values[r] + uppers[r] * result
            conc_in[:, r, where] = jnp.where(live, result, 0.0)

    def write(index):
        where = rows_of(index)
        return pltpu.make_async_copy(
            conc_in.at[:, :, where], conc_new.at[0, :, :, where], out_sem.at[index]
        )

    for load in loads:
        load.wait()
    for offset in [0] + offsets:
        other = peer_of(sub, offset, subs)
        if offset:
            heat_copy(other, sub, other).wait_recv()
        particle(rows_of(other))
        write(other).start()

    @pl.when(sub > 0)
    def _():
        to_above.wait_recv()

    @pl.when(sub == 0)
    def _():
        low_edge[...] = heat[0, :, pl.ds(0, 1)]

    @pl.when(sub < subs - 1)
    def _():
        to_below.wait_recv()

    @pl.when(sub == subs - 1)
    def _():
        high_edge[...] = heat[0, :, pl.ds(rows - 1, 1)]

    for offset in range(1, cells):
        other = peer_of(cell, offset, cells)
        for copy in face_copies(other, other):
            copy.wait_recv()

    row_index = lax.broadcasted_iota(jnp.int32, (rows, gx), 0)
    lane_index = lax.broadcasted_iota(jnp.int32, (rows, gx), 1)

    def fill(layer, carry):
        here = heat[0, layer]
        up = pltpu.roll(here, 1, 0)
        up = jnp.where(row_index == 0, low_edge[layer], up)
        down = pltpu.roll(here, rows - 1, 0)
        down = jnp.where(row_index == rows - 1, high_edge[layer], down)
        left = jnp.where(lane_index == 0, here, pltpu.roll(here, 1, 1))
        right = jnp.where(lane_index == gx - 1, here, pltpu.roll(here, gx - 1, 1))
        laplace = down + up + right + left - 4.0 * here
        base[layer] = here + INPLANE_CONDUCT * laplace
        return carry

    lax.fori_loop(0, layers, fill, jnp.int32(0), unroll=2)
    lower = contacts[cell, 0]
    upper = contacts[cell, 1]
    below_face = jnp.where(lower >= 0, faces[jnp.maximum(lower, 0), 1], 0.0)
    above_face = jnp.where(upper >= 0, faces[jnp.maximum(upper, 0), 0], 0.0)
    base[0] = base[0] + CONTACT_CONDUCT * (below_face - heat[0, 0])
    base[layers - 1] = base[layers - 1] + CONTACT_CONDUCT * (above_face - heat[0, layers - 1])

    for offset in [0] + offsets:
        other = peer_of(sub, offset, subs)
        if offset:
            surf_copy(other, sub, other).wait_recv()
            curr_copy(other, sub, other).wait_recv()
        else:
            for copy in mine:
                copy.wait()
        at = slots_of(other)
        rise = staged[at]
        source, slope = kinetics(surface_rows[at], rise, current_rows[at])
        extra[at] = source - slope * rise
        diagonal[at] = 1.0 - slope

    def row_of(layer):
        slot = layer_slot[layer]
        ends = (layer > 0) + (layer < layers - 1)
        return diagonal[slot] + ends * THROUGH_CONDUCT, base[layer] + extra[slot]

    def sweep(order):
        factors, values = [], []
        for layer in order:
            pivot, right = row_of(layer)
            if factors:
                pivot = pivot - THROUGH_CONDUCT * factors[-1]
                right = right + THROUGH_CONDUCT * values[-1]
            inverse = 1.0 / pivot
            factors.append(THROUGH_CONDUCT * inverse)
            values.append(right * inverse)
        return factors, values

    middle = layers // 2
    low_f, low_v = sweep(range(middle))
    high_f, high_v = sweep(range(layers - 1, middle - 1, -1))
    low = (low_v[-1] + low_f[-1] * high_v[-1]) / (1.0 - low_f[-1] * high_f[-1])
    high = high_v[-1] + high_f[-1] * low
    heat_new[0, middle - 1] = low
    heat_new[0, middle] = high
    for step in range(middle - 2, -1, -1):
        low = low_v[step] + low_f[step] * low
        heat_new[0, step] = low
    for step in range(len(high_v) - 2, -1, -1):
        high = high_v[step] + high_f[step] * high
        heat_new[0, layers - 1 - step] = high

    for copy in sends:
        copy.wait_send()

    @pl.when(sub > 0)
    def _():
        to_below.wait_send()

    @pl.when(sub < subs - 1)
    def _():
        to_above.wait_send()

    for index in range(subs):
        write(index).wait()


def per_device(cells, subs, shell_conc, heat_rise, layer_current, layer_counts, contacts):
    _, slots, shells, gy, gx = shell_conc.shape
    _, layers, rows, _ = heat_rise.shape
    f32 = jnp.float32
    dma = pltpu.SemaphoreType.DMA
    conc_new, heat_new = pl.pallas_call(
        functools.partial(kernel, cells, subs),
        out_shape=(
            jax.ShapeDtypeStruct(shell_conc.shape, f32),
            jax.ShapeDtypeStruct(heat_rise.shape, f32),
        ),
        in_specs=[
            pl.BlockSpec(memory_space=pltpu.SMEM),
            pl.BlockSpec(memory_space=pltpu.SMEM),
            pl.BlockSpec(memory_space=pltpu.VMEM),
            pl.BlockSpec(memory_space=pl.ANY),
            pl.BlockSpec(memory_space=pl.ANY),
        ],
        out_specs=(
            pl.BlockSpec(memory_space=pl.ANY),
            pl.BlockSpec(memory_space=pltpu.VMEM),
        ),
        scratch_shapes=[
            pltpu.VMEM((subs * slots, rows, gx), f32),
            pltpu.VMEM((slots, gy, gx), f32),
            pltpu.VMEM((slots, shells, gy, gx), f32),
            pltpu.VMEM((slots, gy, gx), f32),
            pltpu.VMEM((subs * slots, rows, gx), f32),
            pltpu.VMEM((subs * slots, rows, gx), f32),
            pltpu.VMEM((layers, 1, gx), f32),
            pltpu.VMEM((layers, 1, gx), f32),
            pltpu.VMEM((cells, 2, rows, gx), f32),
            pltpu.VMEM((layers, rows, gx), f32),
            pltpu.VMEM((subs * slots, rows, gx), f32),
            pltpu.VMEM((subs * slots, rows, gx), f32),
            pltpu.SMEM((layers,), jnp.int32),
            dma((4,)),
            dma((subs,)),
            dma((subs,)),
            dma((subs,)),
            dma((subs,)),
            dma((subs,)),
            dma((subs,)),
            dma((2,)),
            dma((2,)),
            dma((2 * cells,)),
            dma((2 * cells,)),
            dma((subs,)),
        ],
        compiler_params=pltpu.CompilerParams(collective_id=0, has_side_effects=True),
    )(layer_counts, contacts, heat_rise, shell_conc, layer_current)
    return conc_new, heat_new


def solution(mesh):
    in_specs = (
        P("cell", "sub", None, None, None),
        P("cell", None, "sub", None),
        P("cell", "sub", None, None),
        P(),
        P(),
    )
    out_specs = (P("cell", "sub", None, None, None), P("cell", None, "sub", None))
    body = functools.partial(per_device, mesh.shape["cell"], mesh.shape["sub"])
    return jax.shard_map(
        body, mesh=mesh, in_specs=in_specs, out_specs=out_specs, check_vma=False
    )
```

time: 72.6 us -> 33.5 us (0.46)
  Pallas kernels: 0 us -> 27 us
  starting transfers between devices: 19.2 us -> 0 us
  local copies, waits for them, and re-layouts: 20 us -> 5.61 us
  other arithmetic: 10.6 us -> 0 us
  waiting for transfers between devices: 10 us -> 0 us
  blocking collectives: 8.23 us -> 0 us
  between operations: 3.8 us -> 0.65 us
    pallas_call x0 -> x1, Pallas kernels: none -> 27 us  [per_device(): pl.pallas_call(functools.partial(kernel, cells, subs), out_shape=(jax.Sha...]
    all_to_all x3 -> x0, starting transfers between devices: 14.9 us -> none  [the longest x1 6.35 us: per_device(): lax.all_to_all(outgoing, 'sub', split_axis=1, concat_axis=2, tiled=True)]
    all_to_all x3 -> x0, waiting for transfers between devices: 9.99 us -> none  [the longest x1 5.76 us: per_device(): lax.all_to_all(source, 'sub', split_axis=2, concat_axis=1, tiled=True)]
    all_gather x1 -> x0, blocking collectives: 8.23 us -> none  [per_device(): every_face = lax.all_gather(face_rows, 'cell', axis=0, tiled=True)]
    mul x11 -> x0, local copies, waits for them, and re-layouts: 7.76 us -> none  [the longest x9 5.07 us: particle(): DIFFUSION_STEP * speedup * ((radial + 1) ** 2 / shells ** 2 * shells)]
    ppermute x2 -> x0, starting transfers between devices: 4.32 us -> none  [the longest x1 3.03 us: with_halo(): lax.ppermute(tail, axis, [(i, (i + 1) % count) for i in range(ends)])]
    slice x4 -> x0, local copies, waits for them, and re-layouts: 4.15 us -> none  [the longest x1 1.9 us: per_device(): row_pad = jnp.pad(heat_rise, ((0, 0), (0, 0), (0, 0), (1, 1)), mode='edge')]
    select_n x6 -> x0, other arithmetic: 3.02 us -> none  [the longest x1 1.84 us: per_device(): conc_new = jnp.where(own_live[None, :, None, None, None], updated, 0.0)]
  transfers between devices with their start and end apart: 5 -> 0, of which waited for: 2 -> 0; matrix products, arithmetic and copies ran while one was open for 26% -> 0% of each run, Pallas kernels for 0% -> 0%
where the time goes in v1:
time: 33.5 us; the launch traced here: 33.3 us
  Pallas kernels  27 us (81%)
  local copies, waits for them, and re-layouts  5.61 us (17%)
  between operations  0.65 us (2%)
    pallas_call x1, Pallas kernels, per_device(): pl.pallas_call(functools.partial(kernel, cells, subs), out_shape=(jax.Sha...  27 us
    unnamed x5, local copies, waits for them, and re-layouts  5.61 us

profile of v1, /device:TPU:0, one launch (start us, length us, event | category | flops | bytes accessed | tf_op | source)
XLA Modules:
  0.0 33.3 jit_solution(8065384775679302826)
XLA Ops:
  0.6 1.3 %copy.7.contacts = s32[4,2]{1,0:T(4,128)} copy(s32[4,2]{0,1:T(2,128)} %param.9) | data formatting | bytes 64 | tf_op args[4]
  2.0 27.0 %shard_map.68 = (f32[1,4,10,128,128]{4,3,2,1,0:T(8,128)}, f32[1,30,16,128]{3,2,1,0:T(8,128)}) custom-call(s32[8]{0:T(128)} %counts.1, s32[4,2]{1,0:T(4,128)} %copy.7.contacts, f32[1,30,16,128]{3,2,1,0:T(8,128)} %heat.1, f32[1,4,10,128,128]{4,3,2,1,0:T(8,128)} %conc.1, f32[1,4,128,128]{3,2,1,0:T(8,128)} %current.1), custom_call_target="tpu_custom_call" | custom-call | tf_op jit(solution)/shard_map/pallas_call | solution.py:391
  29.0 0.0 copy-start
  29.0 3.6 %copy.10 = f32[1,4,10,128,128]{4,3,2,1,0:T(8,128)} copy(f32[1,4,10,128,128]{4,3,2,1,0:T(8,128)} %get-tuple-element.4) | data formatting | bytes 5242880
  32.6 0.0 copy-done
  32.6 0.7 %copy.11 = f32[1,30,16,128]{3,2,1,0:T(8,128)} copy(f32[1,30,16,128]{3,2,1,0:T(8,128)S(1)} %copy-done) | data formatting | bytes 491520
Async XLA Ops:
  29.0 3.6 %copy-start = (f32[1,30,16,128]{3,2,1,0:T(8,128)S(1)}, f32[1,30,16,128]{3,2,1,0:T(8,128)}, u32[]{:S(2)}) copy-start(f32[1,30,16,128]{3,2,1,0:T(8,128)} %get-tuple-element.5) | copy-start | bytes 737284

commit v2 on v1

--- a/solution.py
+++ b/solution.py
@@ -20,6 +20,7 @@
 THROUGH_CONDUCT = 2.0
 CONTACT_CONDUCT = 0.5
 MESH = pl.DeviceIdType.MESH
+GRANT = 24 << 20
 
 
 def partner(me, offset):
@@ -68,12 +69,12 @@
 
 def kernel(
     cells, subs,
-    counts, contacts, heat, conc, current,
-    conc_new, heat_new,
-    staged, slot_rise, conc_in, current_in, surface_rows, current_rows,
+    counts, contacts, heat_hbm, conc, current,
+    conc_in, right_side, pivots,
+    heat, staged, slot_rise, current_in, surface_rows, current_rows,
     low_edge, high_edge, faces, base, extra, diagonal, layer_slot,
     own_sem, heat_send, heat_recv, surf_send, surf_recv, curr_send, curr_recv,
-    edge_send, edge_recv, face_send, face_recv, out_sem,
+    edge_send, edge_recv, face_send, face_recv,
 ):
     cell = lax.axis_index("cell")
     sub = lax.axis_index("sub")
@@ -86,6 +87,8 @@
     def at_sub(index):
         return (cell, index)
 
+    heat_load = pltpu.make_async_copy(heat_hbm, heat, own_sem.at[4])
+    heat_load.start()
     barrier = pltpu.get_barrier_semaphore()
     for offset in offsets:
         pl.semaphore_signal(
@@ -103,6 +106,7 @@
     for load in loads:
         load.start()
 
+    heat_load.wait()
     start = jnp.int32(0)
     for index in range(subs):
         held = counts[index]
@@ -168,7 +172,7 @@
         sends.append(copy)
 
     to_below = pltpu.make_async_remote_copy(
-        src_ref=heat.at[0, :, pl.ds(0, 1)],
+        src_ref=heat_hbm.at[0, :, pl.ds(0, 1)],
         dst_ref=high_edge,
         send_sem=edge_send.at[0],
         recv_sem=edge_recv.at[0],
@@ -176,7 +180,7 @@
         device_id_type=MESH,
     )
     to_above = pltpu.make_async_remote_copy(
-        src_ref=heat.at[0, :, pl.ds(rows - 1, 1)],
+        src_ref=heat_hbm.at[0, :, pl.ds(rows - 1, 1)],
         dst_ref=low_edge,
         send_sem=edge_send.at[1],
         recv_sem=edge_recv.at[1],
@@ -195,7 +199,7 @@
     def face_copies(source, device):
         return [
             pltpu.make_async_remote_copy(
-                src_ref=heat.at[0, layer],
+                src_ref=heat_hbm.at[0, layer],
                 dst_ref=faces.at[source, place],
                 send_sem=face_send.at[2 * device + place],
                 recv_sem=face_recv.at[2 * source + place],
@@ -264,12 +268,6 @@
             result = values[r] + uppers[r] * result
             conc_in[:, r, where] = jnp.where(live, result, 0.0)
 
-    def write(index):
-        where = rows_of(index)
-        return pltpu.make_async_copy(
-            conc_in.at[:, :, where], conc_new.at[0, :, :, where], out_sem.at[index]
-        )
-
     for load in loads:
         load.wait()
     for offset in [0] + offsets:
@@ -277,7 +275,6 @@
         if offset:
             heat_copy(other, sub, other).wait_recv()
         particle(rows_of(other))
-        write(other).start()
 
     @pl.when(sub > 0)
     def _():
@@ -316,8 +313,8 @@
         return carry
 
     lax.fori_loop(0, layers, fill, jnp.int32(0), unroll=2)
-    lower = contacts[cell, 0]
-    upper = contacts[cell, 1]
+    lower = contacts[0, cell]
+    upper = contacts[1, cell]
     below_face = jnp.where(lower >= 0, faces[jnp.maximum(lower, 0), 1], 0.0)
     above_face = jnp.where(upper >= 0, faces[jnp.maximum(upper, 0), 0], 0.0)
     base[0] = base[0] + CONTACT_CONDUCT * (below_face - heat[0, 0])
@@ -337,15 +334,37 @@
         extra[at] = source - slope * rise
         diagonal[at] = 1.0 - slope
 
-    def row_of(layer):
+    for layer in range(layers):
         slot = layer_slot[layer]
         ends = (layer > 0) + (layer < layers - 1)
-        return diagonal[slot] + ends * THROUGH_CONDUCT, base[layer] + extra[slot]
+        pivots[layer] = diagonal[slot] + ends * THROUGH_CONDUCT
+        right_side[layer] = base[layer] + extra[slot]
+
+    for copy in sends:
+        copy.wait_send()
+
+    @pl.when(sub > 0)
+    def _():
+        to_below.wait_send()
+
+    @pl.when(sub < subs - 1)
+    def _():
+        to_above.wait_send()
+
+
+def finish(conc, right_side, pivots, conc_new, heat_new, sem):
+    slots = conc.shape[0]
+    layers = right_side.shape[0]
+    writes = [
+        pltpu.make_async_copy(conc.at[s], conc_new.at[0, s], sem.at[s]) for s in range(slots)
+    ]
+    for write in writes:
+        write.start()
 
     def sweep(order):
         factors, values = [], []
         for layer in order:
-            pivot, right = row_of(layer)
+            pivot, right = pivots[layer], right_side[layer]
             if factors:
                 pivot = pivot - THROUGH_CONDUCT * factors[-1]
                 right = right + THROUGH_CONDUCT * values[-1]
@@ -367,20 +386,8 @@
     for step in range(len(high_v) - 2, -1, -1):
         high = high_v[step] + high_f[step] * high
         heat_new[0, layers - 1 - step] = high
-
-    for copy in sends:
-        copy.wait_send()
-
-    @pl.when(sub > 0)
-    def _():
-        to_below.wait_send()
-
-    @pl.when(sub < subs - 1)
-    def _():
-        to_above.wait_send()
-
-    for index in range(subs):
-        write(index).wait()
+    for write in writes:
+        write.wait()
 
 
 def per_device(cells, subs, shell_conc, heat_rise, layer_current, layer_counts, contacts):
@@ -388,38 +395,37 @@
     _, layers, rows, _ = heat_rise.shape
     f32 = jnp.float32
     dma = pltpu.SemaphoreType.DMA
-    conc_new, heat_new = pl.pallas_call(
+    table = (layers, rows, gx)
+    conc, right_side, pivots = pl.pallas_call(
         functools.partial(kernel, cells, subs),
         out_shape=(
-            jax.ShapeDtypeStruct(shell_conc.shape, f32),
-            jax.ShapeDtypeStruct(heat_rise.shape, f32),
+            pltpu.VMEM((slots, shells, gy, gx), f32),
+            pltpu.VMEM(table, f32),
+            pltpu.VMEM(table, f32),
         ),
         in_specs=[
             pl.BlockSpec(memory_space=pltpu.SMEM),
             pl.BlockSpec(memory_space=pltpu.SMEM),
-            pl.BlockSpec(memory_space=pltpu.VMEM),
-            pl.BlockSpec(memory_space=pl.ANY),
-            pl.BlockSpec(memory_space=pl.ANY),
+            pl.BlockSpec(memory_space=pltpu.HBM),
+            pl.BlockSpec(memory_space=pltpu.HBM),
+            pl.BlockSpec(memory_space=pltpu.HBM),
         ],
-        out_specs=(
-            pl.BlockSpec(memory_space=pl.ANY),
-            pl.BlockSpec(memory_space=pltpu.VMEM),
-        ),
+        out_specs=(pl.BlockSpec(memory_space=pltpu.VMEM),) * 3,
         scratch_shapes=[
+            pltpu.VMEM(heat_rise.shape, f32),
             pltpu.VMEM((subs * slots, rows, gx), f32),
             pltpu.VMEM((slots, gy, gx), f32),
-            pltpu.VMEM((slots, shells, gy, gx), f32),
             pltpu.VMEM((slots, gy, gx), f32),
             pltpu.VMEM((subs * slots, rows, gx), f32),
             pltpu.VMEM((subs * slots, rows, gx), f32),
             pltpu.VMEM((layers, 1, gx), f32),
             pltpu.VMEM((layers, 1, gx), f32),
             pltpu.VMEM((cells, 2, rows, gx), f32),
-            pltpu.VMEM((layers, rows, gx), f32),
+            pltpu.VMEM(table, f32),
             pltpu.VMEM((subs * slots, rows, gx), f32),
             pltpu.VMEM((subs * slots, rows, gx), f32),
             pltpu.SMEM((layers,), jnp.int32),
-            dma((4,)),
+            dma((5,)),
             dma((subs,)),
             dma((subs,)),
             dma((subs,)),
@@ -430,10 +436,25 @@
             dma((2,)),
             dma((2 * cells,)),
             dma((2 * cells,)),
-            dma((subs,)),
         ],
-        compiler_params=pltpu.CompilerParams(collective_id=0, has_side_effects=True),
-    )(layer_counts, contacts, heat_rise, shell_conc, layer_current)
+        compiler_params=pltpu.CompilerParams(
+            collective_id=0, has_side_effects=True, vmem_limit_bytes=GRANT
+        ),
+    )(layer_counts, contacts.T, heat_rise, shell_conc, layer_current)
+    conc_new, heat_new = pl.pallas_call(
+        finish,
+        out_shape=(
+            jax.ShapeDtypeStruct(shell_conc.shape, f32),
+            jax.ShapeDtypeStruct(heat_rise.shape, f32),
+        ),
+        in_specs=[pl.BlockSpec(memory_space=pltpu.VMEM)] * 3,
+        out_specs=(
+            pl.BlockSpec(memory_space=pl.ANY),
+            pl.BlockSpec(memory_space=pltpu.VMEM),
+        ),
+        scratch_shapes=[dma((slots,))],
+        compiler_params=pltpu.CompilerParams(vmem_limit_bytes=GRANT),
+    )(conc, right_side, pivots)
     return conc_new, heat_new
 
 

time: 33.5 us -> 34.1 us (1.018)
  Pallas kernels: 27 us -> 28.2 us
  local copies, waits for them, and re-layouts: 5.61 us -> 4.96 us
    pallas_call x1 -> x2, Pallas kernels: 27 us -> 28.2 us  [the longest x1 26 us: per_device(): pl.pallas_call(functools.partial(kernel, cells, subs), out_shape=(pltpu.V...]
    unnamed x5 -> x10, local copies, waits for them, and re-layouts: 5.61 us -> 4.96 us
where the time goes in v2:
time: 34.1 us; the launch traced here: 33.8 us
  Pallas kernels  28.2 us (83%)
  local copies, waits for them, and re-layouts  4.96 us (15%)
  between operations  0.65 us (2%)
    pallas_call x1, Pallas kernels, per_device(): pl.pallas_call(functools.partial(kernel, cells, subs), out_shape=(pltpu.V...  26 us
    unnamed x10, local copies, waits for them, and re-layouts  4.96 us
    pallas_call x1, Pallas kernels, per_device(): pl.pallas_call(finish, out_shape=(jax.ShapeDtypeStruct(shell_conc.shape,...  2.21 us

profile of v2, /device:TPU:0, one launch (start us, length us, event | category | flops | bytes accessed | tf_op | source)
XLA Modules:
  0.0 33.8 jit_solution(472520344293295627)
XLA Ops:
  0.6 0.0 copy-start
  0.6 1.7 %copy-done = f32[1,4,10,128,128]{4,3,2,1,0:T(8,128)S(1)} copy-done((f32[1,4,10,128,128]{4,3,2,1,0:T(8,128)S(1)}, f32[1,4,10,128,128]{4,3,2,1,0:T(8,128)}, u32[]{:S(2)}) %copy-start) | copy-done | bytes 2621464
  2.4 0.0 copy-start.1
  2.4 0.9 %copy-done.1 = f32[1,4,128,128]{3,2,1,0:T(8,128)S(1)} copy-done((f32[1,4,128,128]{3,2,1,0:T(8,128)S(1)}, f32[1,4,128,128]{3,2,1,0:T(8,128)}, u32[]{:S(2)}) %copy-start.1) | copy-done | bytes 262168
  3.3 0.0 copy-start.2
  3.3 0.9 %copy-done.2 = f32[1,30,16,128]{3,2,1,0:T(8,128)S(1)} copy-done((f32[1,30,16,128]{3,2,1,0:T(8,128)S(1)}, f32[1,30,16,128]{3,2,1,0:T(8,128)}, u32[]{:S(2)}) %copy-start.2) | copy-done | bytes 245784
  4.3 0.0 copy-start.3
  4.3 0.7 %copy-done.3 = s32[4,2]{0,1:T(2,128)S(1)} copy-done((s32[4,2]{0,1:T(2,128)S(1)}, s32[4,2]{0,1:T(2,128)}, u32[]{:S(2)}) %copy-start.3) | copy-done | bytes 56
  4.9 0.0 copy-start.4
  4.9 0.7 %copy-done.4 = s32[8]{0:T(128)S(1)} copy-done((s32[8]{0:T(128)S(1)}, s32[8]{0:T(128)}, u32[]{:S(2)}) %copy-start.4) | copy-done | bytes 56
  5.6 26.0 %shard_map.68 = (f32[4,10,128,128]{3,2,1,0:T(8,128)S(1)}, f32[30,16,128]{2,1,0:T(8,128)S(1)}, f32[30,16,128]{2,1,0:T(8,128)S(1)}) custom-call(s32[8]{0:T(128)S(1)} %copy-done.4, s32[2,4]{1,0:T(2,128)S(1)} %bitcast.1, f32[1,30,16,128]{3,2,1,0:T(8,128)S(1)} %copy-done.2, f32[1,4,10,128,128]{4,3,2,1,0:T(8,128)S(1)} %copy-done, f32[1,4,128,128]{3,2,1,0:T(8,128)S(1)} %copy-done.1), custom_call_target="tpu_custom_call" | custom-call | tf_op jit(solution)/shard_map/pallas_call | solution.py:399
  31.6 2.2 %shard_map.69 = (f32[1,4,10,128,128]{4,3,2,1,0:T(8,128)}, f32[1,30,16,128]{3,2,1,0:T(8,128)}) custom-call(f32[4,10,128,128]{3,2,1,0:T(8,128)S(1)} %get-tuple-element.5.conc, f32[30,16,128]{2,1,0:T(8,128)S(1)} %get-tuple-element.6.right_side, f32[30,16,128]{2,1,0:T(8,128)S(1)} %get-tuple-element.7.pivots), custom_call_target="tpu_custom_call" | custom-call | tf_op jit(solution)/shard_map/pallas_call | solution.py:444
Async XLA Ops:
  0.6 1.7 %copy-start = (f32[1,4,10,128,128]{4,3,2,1,0:T(8,128)S(1)}, f32[1,4,10,128,128]{4,3,2,1,0:T(8,128)}, u32[]{:S(2)}) copy-start(f32[1,4,10,128,128]{4,3,2,1,0:T(8,128)} %conc.1) | copy-start | bytes 7864324
  2.4 0.9 %copy-start.1 = (f32[1,4,128,128]{3,2,1,0:T(8,128)S(1)}, f32[1,4,128,128]{3,2,1,0:T(8,128)}, u32[]{:S(2)}) copy-start(f32[1,4,128,128]{3,2,1,0:T(8,128)} %current.1) | copy-start | bytes 786436
  3.3 0.9 %copy-start.2 = (f32[1,30,16,128]{3,2,1,0:T(8,128)S(1)}, f32[1,30,16,128]{3,2,1,0:T(8,128)}, u32[]{:S(2)}) copy-start(f32[1,30,16,128]{3,2,1,0:T(8,128)} %heat_hbm.1) | copy-start | bytes 737284
  4.3 0.7 %copy-start.3 = (s32[4,2]{0,1:T(2,128)S(1)}, s32[4,2]{0,1:T(2,128)}, u32[]{:S(2)}) copy-start(s32[4,2]{0,1:T(2,128)} %param.9) | copy-start | bytes 100
  4.9 0.7 %copy-start.4 = (s32[8]{0:T(128)S(1)}, s32[8]{0:T(128)}, u32[]{:S(2)}) copy-start(s32[8]{0:T(128)} %counts.1) | copy-start | bytes 100

commit v3 on v2

--- a/solution.py
+++ b/solution.py
@@ -69,10 +69,10 @@
 
 def kernel(
     cells, subs,
-    counts, contacts, heat_hbm, conc, current,
+    counts_hbm, contacts_hbm, heat_hbm, conc, current,
     conc_in, right_side, pivots,
     heat, staged, slot_rise, current_in, surface_rows, current_rows,
-    low_edge, high_edge, faces, base, extra, diagonal, layer_slot,
+    low_edge, high_edge, faces, base, extra, diagonal, layer_slot, counts, contacts,
     own_sem, heat_send, heat_recv, surf_send, surf_recv, curr_send, curr_recv,
     edge_send, edge_recv, face_send, face_recv,
 ):
@@ -87,8 +87,13 @@
     def at_sub(index):
         return (cell, index)
 
-    heat_load = pltpu.make_async_copy(heat_hbm, heat, own_sem.at[4])
-    heat_load.start()
+    first_loads = [
+        pltpu.make_async_copy(counts_hbm, counts, own_sem.at[5]),
+        pltpu.make_async_copy(heat_hbm, heat, own_sem.at[4]),
+        pltpu.make_async_copy(contacts_hbm, contacts, own_sem.at[6]),
+    ]
+    for load in first_loads:
+        load.start()
     barrier = pltpu.get_barrier_semaphore()
     for offset in offsets:
         pl.semaphore_signal(
@@ -106,7 +111,8 @@
     for load in loads:
         load.start()
 
-    heat_load.wait()
+    for load in first_loads:
+        load.wait()
     start = jnp.int32(0)
     for index in range(subs):
         held = counts[index]
@@ -396,6 +402,10 @@
     f32 = jnp.float32
     dma = pltpu.SemaphoreType.DMA
     table = (layers, rows, gx)
+    held = [
+        pltpu.with_memory_space_constraint(array, pltpu.HBM)
+        for array in (layer_counts, contacts.T, heat_rise, shell_conc, layer_current)
+    ]
     conc, right_side, pivots = pl.pallas_call(
         functools.partial(kernel, cells, subs),
         out_shape=(
@@ -404,12 +414,8 @@
             pltpu.VMEM(table, f32),
         ),
         in_specs=[
-            pl.BlockSpec(memory_space=pltpu.SMEM),
-            pl.BlockSpec(memory_space=pltpu.SMEM),
-            pl.BlockSpec(memory_space=pltpu.HBM),
-            pl.BlockSpec(memory_space=pltpu.HBM),
-            pl.BlockSpec(memory_space=pltpu.HBM),
-        ],
+            pl.BlockSpec(memory_space=pltpu.HBM)
+        ] * 5,
         out_specs=(pl.BlockSpec(memory_space=pltpu.VMEM),) * 3,
         scratch_shapes=[
             pltpu.VMEM(heat_rise.shape, f32),
@@ -425,7 +431,9 @@
             pltpu.VMEM((subs * slots, rows, gx), f32),
             pltpu.VMEM((subs * slots, rows, gx), f32),
             pltpu.SMEM((layers,), jnp.int32),
-            dma((5,)),
+            pltpu.SMEM(layer_counts.shape, jnp.int32),
+            pltpu.SMEM(contacts.shape[::-1], jnp.int32),
+            dma((7,)),
             dma((subs,)),
             dma((subs,)),
             dma((subs,)),
@@ -440,7 +448,7 @@
         compiler_params=pltpu.CompilerParams(
             collective_id=0, has_side_effects=True, vmem_limit_bytes=GRANT
         ),
-    )(layer_counts, contacts.T, heat_rise, shell_conc, layer_current)
+    )(*held)
     conc_new, heat_new = pl.pallas_call(
         finish,
         out_shape=(

time: 34.1 us -> 28.2 us (0.83)
  local copies, waits for them, and re-layouts: 4.96 us -> 0 us
  Pallas kernels: 28.2 us -> 27.4 us
    unnamed x10 -> x0, local copies, waits for them, and re-layouts: 4.96 us -> none
    pallas_call x1, Pallas kernels: 26 us -> 25.2 us  [per_device(): pl.pallas_call(functools.partial(kernel, cells, subs), out_shape=(pltpu.V...]
where the time goes in v3:
time: 28.2 us; the launch traced here: 28 us
  Pallas kernels  27.4 us (97%)
  between operations  0.64 us (2%)
    pallas_call x1, Pallas kernels, per_device(): pl.pallas_call(functools.partial(kernel, cells, subs), out_shape=(pltpu.V...  25.2 us
    pallas_call x1, Pallas kernels, per_device(): pl.pallas_call(finish, out_shape=(jax.ShapeDtypeStruct(shell_conc.shape,...  2.21 us

profile of v3, /device:TPU:0, one launch (start us, length us, event | category | flops | bytes accessed | tf_op | source)
XLA Modules:
  0.0 28.0 jit_solution(7934726348296716191)
XLA Ops:
  0.6 25.2 %shard_map.68 = (f32[4,10,128,128]{3,2,1,0:T(8,128)S(1)}, f32[30,16,128]{2,1,0:T(8,128)S(1)}, f32[30,16,128]{2,1,0:T(8,128)S(1)}) custom-call(s32[8]{0:T(128)} %counts_hbm.1, s32[2,4]{1,0:T(2,128)} %bitcast.1, f32[1,30,16,128]{3,2,1,0:T(8,128)} %heat_hbm.1, f32[1,4,10,128,128]{4,3,2,1,0:T(8,128)} %conc.1, f32[1,4,128,128]{3,2,1,0:T(8,128)} %current.1), custom_call_target="tpu_custom_call" | custom-call | tf_op jit(solution)/shard_map/pallas_call | solution.py:409
  25.8 2.2 %shard_map.69 = (f32[1,4,10,128,128]{4,3,2,1,0:T(8,128)}, f32[1,30,16,128]{3,2,1,0:T(8,128)}) custom-call(f32[4,10,128,128]{3,2,1,0:T(8,128)S(1)} %get-tuple-element.5.conc, f32[30,16,128]{2,1,0:T(8,128)S(1)} %get-tuple-element.6.right_side, f32[30,16,128]{2,1,0:T(8,128)S(1)} %get-tuple-element.7.pivots), custom_call_target="tpu_custom_call" | custom-call | tf_op jit(solution)/shard_map/pallas_call | solution.py:452

commit v4 on v3

--- a/solution.py
+++ b/solution.py
@@ -72,7 +72,7 @@
     counts_hbm, contacts_hbm, heat_hbm, conc, current,
     conc_in, right_side, pivots,
     heat, staged, slot_rise, current_in, surface_rows, current_rows,
-    low_edge, high_edge, faces, base, extra, diagonal, layer_slot, counts, contacts,
+    edges, low_edge, high_edge, faces, base, extra, diagonal, layer_slot, counts, contacts,
     own_sem, heat_send, heat_recv, surf_send, surf_recv, curr_send, curr_recv,
     edge_send, edge_recv, face_send, face_recv,
 ):
@@ -113,6 +113,8 @@
 
     for load in first_loads:
         load.wait()
+    edges[0] = heat[0, :, 0]
+    edges[1] = heat[0, :, rows - 1]
     start = jnp.int32(0)
     for index in range(subs):
         held = counts[index]
@@ -177,8 +179,13 @@
         copy.start()
         sends.append(copy)
 
+    for offset in far_first:
+        other = peer_of(sub, offset, subs)
+        for copy in (surf_copy(sub, other, other), curr_copy(sub, other, other)):
+            copy.start()
+            sends.append(copy)
     to_below = pltpu.make_async_remote_copy(
-        src_ref=heat_hbm.at[0, :, pl.ds(0, 1)],
+        src_ref=edges.at[0],
         dst_ref=high_edge,
         send_sem=edge_send.at[0],
         recv_sem=edge_recv.at[0],
@@ -186,7 +193,7 @@
         device_id_type=MESH,
     )
     to_above = pltpu.make_async_remote_copy(
-        src_ref=heat_hbm.at[0, :, pl.ds(rows - 1, 1)],
+        src_ref=edges.at[1],
         dst_ref=low_edge,
         send_sem=edge_send.at[1],
         recv_sem=edge_recv.at[1],
@@ -220,11 +227,6 @@
             copy.start()
             sends.append(copy)
 
-    for offset in far_first:
-        other = peer_of(sub, offset, subs)
-        for copy in (surf_copy(sub, other, other), curr_copy(sub, other, other)):
-            copy.start()
-            sends.append(copy)
     mine = [
         pltpu.make_async_copy(
             conc.at[0, :, shells - 1, rows_of(sub)], surface_rows.at[slots_of(sub)], own_sem.at[2]
@@ -288,7 +290,7 @@
 
     @pl.when(sub == 0)
     def _():
-        low_edge[...] = heat[0, :, pl.ds(0, 1)]
+        low_edge[...] = edges[0]
 
     @pl.when(sub < subs - 1)
     def _():
@@ -296,7 +298,7 @@
 
     @pl.when(sub == subs - 1)
     def _():
-        high_edge[...] = heat[0, :, pl.ds(rows - 1, 1)]
+        high_edge[...] = edges[1]
 
     for offset in range(1, cells):
         other = peer_of(cell, offset, cells)
@@ -309,9 +311,9 @@
     def fill(layer, carry):
         here = heat[0, layer]
         up = pltpu.roll(here, 1, 0)
-        up = jnp.where(row_index == 0, low_edge[layer], up)
+        up = jnp.where(row_index == 0, low_edge[pl.ds(layer, 1)], up)
         down = pltpu.roll(here, rows - 1, 0)
-        down = jnp.where(row_index == rows - 1, high_edge[layer], down)
+        down = jnp.where(row_index == rows - 1, high_edge[pl.ds(layer, 1)], down)
         left = jnp.where(lane_index == 0, here, pltpu.roll(here, 1, 1))
         right = jnp.where(lane_index == gx - 1, here, pltpu.roll(here, gx - 1, 1))
         laplace = down + up + right + left - 4.0 * here
@@ -326,7 +328,7 @@
     base[0] = base[0] + CONTACT_CONDUCT * (below_face - heat[0, 0])
     base[layers - 1] = base[layers - 1] + CONTACT_CONDUCT * (above_face - heat[0, layers - 1])
 
-    for offset in [0] + offsets:
+    for offset in [0] + far_first:
         other = peer_of(sub, offset, subs)
         if offset:
             surf_copy(other, sub, other).wait_recv()
@@ -424,8 +426,9 @@
             pltpu.VMEM((slots, gy, gx), f32),
             pltpu.VMEM((subs * slots, rows, gx), f32),
             pltpu.VMEM((subs * slots, rows, gx), f32),
-            pltpu.VMEM((layers, 1, gx), f32),
-            pltpu.VMEM((layers, 1, gx), f32),
+            pltpu.VMEM((2, layers, gx), f32),
+            pltpu.VMEM((layers, gx), f32),
+            pltpu.VMEM((layers, gx), f32),
             pltpu.VMEM((cells, 2, rows, gx), f32),
             pltpu.VMEM(table, f32),
             pltpu.VMEM((subs * slots, rows, gx), f32),

time: 28.2 us -> 28 us (level)
  no operation moved by 1% of the time
where the time goes in v4:
time: 28 us; the launch traced here: 27.9 us
  Pallas kernels  27.2 us (97%)
  between operations  0.64 us (2%)
    pallas_call x1, Pallas kernels, per_device(): pl.pallas_call(functools.partial(kernel, cells, subs), out_shape=(pltpu.V...  25 us
    pallas_call x1, Pallas kernels, per_device(): pl.pallas_call(finish, out_shape=(jax.ShapeDtypeStruct(shell_conc.shape,...  2.21 us

profile of v4, /device:TPU:0, one launch (start us, length us, event | category | flops | bytes accessed | tf_op | source)
XLA Modules:
  0.0 27.9 jit_solution(7546387524181654005)
XLA Ops:
  0.6 25.0 %shard_map.68 = (f32[4,10,128,128]{3,2,1,0:T(8,128)S(1)}, f32[30,16,128]{2,1,0:T(8,128)S(1)}, f32[30,16,128]{2,1,0:T(8,128)S(1)}) custom-call(s32[8]{0:T(128)} %counts_hbm.1, s32[2,4]{1,0:T(2,128)} %bitcast.1, f32[1,30,16,128]{3,2,1,0:T(8,128)} %heat_hbm.1, f32[1,4,10,128,128]{4,3,2,1,0:T(8,128)} %conc.1, f32[1,4,128,128]{3,2,1,0:T(8,128)} %current.1), custom_call_target="tpu_custom_call" | custom-call | tf_op jit(solution)/shard_map/pallas_call | solution.py:411
  25.7 2.2 %shard_map.69 = (f32[1,4,10,128,128]{4,3,2,1,0:T(8,128)}, f32[1,30,16,128]{3,2,1,0:T(8,128)}) custom-call(f32[4,10,128,128]{3,2,1,0:T(8,128)S(1)} %get-tuple-element.5.conc, f32[30,16,128]{2,1,0:T(8,128)S(1)} %get-tuple-element.6.right_side, f32[30,16,128]{2,1,0:T(8,128)S(1)} %get-tuple-element.7.pivots), custom_call_target="tpu_custom_call" | custom-call | tf_op jit(solution)/shard_map/pallas_call | solution.py:455
